TPU v7x, 32 devices: a whole 2x2x4 slice. The times are simulated.
32 devices in a mesh: seq: 8 (over z, x), head: 4 (over y, core).
Axes of the slice: x: 2, y: 2, z: 4, core: 2. Of those that a mesh axis runs over, the one named last changes fastest.
Arguments:
- queries: bfloat16 [2048, 2048], P('seq', 'head'), may hold values from -1.75 to 1.75
- keys: bfloat16 [2048, 2048], P('seq', 'head'), may hold values from -1.75 to 1.75
- values: bfloat16 [2048, 2048], P('seq', 'head'), may hold values from -6 to 6
- level_table: float32 [16, 16], P(None, 'head'), may hold values from 0.05 to 1
- level_code: int32 [2048, 6], P('seq'), may hold values from 0 to 15
- out_weight: bfloat16 [2048, 2048], P('head'), may hold values from -0.125 to 0.125
- cotangent: bfloat16 [2048, 2048], P('seq', 'head'), may hold values from -8 to 8
Outputs:
- mixed: bfloat16 [2048, 2048], P('seq', 'head')
- out_weight_grad: float32 [2048, 2048], P('seq', 'head')
- query_grad: bfloat16 [2048, 2048], P('seq', 'head')
- key_grad: bfloat16 [2048, 2048], P('seq', 'head')
- value_grad: bfloat16 [2048, 2048], P('seq', 'head')
- table_grad: float32 [16, 16], P(None, 'head')
All inputs are finite; a program needn't handle non-finite values.
Results may differ from a plain program's by a relative error of at most 0.015.
Values may be sent and summed in bfloat16 or wider, within the bound.
No kernel may reach another device: no remote copies, remote signals or barrier semaphores. Data moves between devices by JAX's collectives and lax.ppermute only.
A program may use at most 128 MiB of HBM per device.

v0:
```python
import math
import jax
import jax.numpy as jnp
from jax import lax
from jax.sharding import PartitionSpec as P

SPAN = 64
HIGHEST_PRECISION = lax.Precision.HIGHEST


def partner_2(value, axis, apart):
    mask = 2**apart
    pairs = [(source, source ^ mask) for source in range(lax.axis_size(axis))]
    return lax.ppermute(value, axis, pairs)


def split_einsum(form, left, right):
    if left.dtype == jnp.float32:
        high = left.astype(jnp.bfloat16)
        rest = (left - high.astype(jnp.float32)).astype(jnp.bfloat16)
        return jnp.einsum(form, high, right, preferred_element_type=jnp.float32) + jnp.einsum(
            form, rest, right, preferred_element_type=jnp.float32
        )
    high = right.astype(jnp.bfloat16)
    rest = (right - high.astype(jnp.float32)).astype(jnp.bfloat16)
    return jnp.einsum(form, left, high, preferred_element_type=jnp.float32) + jnp.einsum(
        form, left, rest, preferred_element_type=jnp.float32
    )


def upper_half(array, bit_index):
    group_size = 2 ** (bit_index + 1)
    grouped = array.reshape((array.shape[0] // group_size, group_size) + array.shape[1:])
    return grouped[:, group_size // 2 :]


def lower_sum(array, bit_index):
    group_size = 2 ** (bit_index + 1)
    grouped = array.reshape((array.shape[0] // group_size, group_size) + array.shape[1:])
    return jnp.sum(grouped[:, : group_size // 2], axis=1)


def place_upper(piece_array, bit_index):
    group_size = 2 ** (bit_index + 1)
    joined = jnp.concatenate([jnp.zeros_like(piece_array), piece_array], axis=1)
    return joined.reshape((piece_array.shape[0] * group_size,) + piece_array.shape[2:])


def spread_lower(piece_array, bit_index):
    group_size = 2 ** (bit_index + 1)
    filled = jnp.broadcast_to(
        piece_array[:, None], (piece_array.shape[0], group_size // 2) + piece_array.shape[1:]
    )
    joined = jnp.concatenate([filled, jnp.zeros_like(filled)], axis=1)
    return joined.reshape((piece_array.shape[0] * group_size,) + piece_array.shape[1:])


def lower_blocks(device_state, position, seq_bits):
    block_state = device_state
    found_states = []
    for bit_index in range(seq_bits):
        partner = partner_2(block_state.astype(jnp.bfloat16), "seq", bit_index).astype(
            block_state.dtype
        )
        bit_owned = (position >> bit_index & 1).astype(jnp.float32)
        found_states.append(partner * bit_owned)
        block_state = block_state + partner
    return found_states


def upper_blocks(device_terms, position, seq_bits):
    stacked_terms = device_terms
    gathered = jnp.zeros_like(device_terms[0])
    for bit_index in range(seq_bits):
        partner = partner_2(stacked_terms.astype(jnp.bfloat16), "seq", bit_index).astype(
            stacked_terms.dtype
        )
        bit_owned = (position >> bit_index & 1).astype(jnp.float32)
        gathered = gathered + (1.0 - bit_owned) * partner[0]
        stacked_terms = stacked_terms[1:] + partner[1:]
    return gathered


def per_device(queries, keys, values, level_table, level_code, out_weight, cotangent):
    tok_rows = queries.shape[0]
    heads_here = level_table.shape[1]
    head_size = queries.shape[1] // heads_here
    span_len = SPAN
    spans_here = tok_rows // span_len
    local_bits = spans_here.bit_length() - 1
    seq_count = lax.axis_size("seq")
    seq_bits = seq_count.bit_length() - 1
    level_count = 1 + local_bits + seq_bits
    position = lax.axis_index("seq")
    four_shape = (spans_here, span_len, heads_here, head_size)
    scales = [
        1.0 / math.sqrt(span_len * 2 ** max(level_index - 1, 0))
        for level_index in range(level_count)
    ]
    code_count = level_table.shape[0]
    one_hot = (
        level_code[:, :, None] == jnp.arange(code_count, dtype=jnp.int32)[None, None, :]
    ).astype(jnp.float32)
    lookup = jnp.einsum("tlc,ch->tlh", one_hot, level_table, precision=HIGHEST_PRECISION)
    lookup = lookup.reshape(spans_here, span_len, level_count, heads_here)
    level_coef = lookup * jnp.asarray(scales, jnp.float32)[None, None, :, None]
    full_rows = lax.all_gather(cotangent, "head", axis=1, tiled=True)
    grad_attn = jnp.einsum(
        "tj,ij->ti", full_rows, out_weight, preferred_element_type=jnp.float32
    ).astype(jnp.bfloat16)
    q_half = queries.reshape(four_shape)
    k_half = keys.reshape(four_shape)
    v_half = values.reshape(four_shape)
    g_half = grad_attn.reshape(four_shape)
    causal = (jnp.arange(span_len)[:, None] >= jnp.arange(span_len)[None, :]).astype(jnp.float32)
    scores = (
        jnp.einsum("jchd,jshd->jhcs", q_half, k_half, preferred_element_type=jnp.float32) * causal
    )
    level_reads = [split_einsum("jhcs,jshe->jche", scores, v_half) * scales[0]]
    span_states = jnp.einsum("jchd,jche->jhde", k_half, v_half, preferred_element_type=jnp.float32)
    local_lower = []
    for bit_index in range(local_bits):
        lower_state = lower_sum(span_states, bit_index)
        local_lower.append(lower_state)
        upper_reads = split_einsum("gjchd,ghde->gjche", upper_half(q_half, bit_index), lower_state)
        level_reads.append(place_upper(upper_reads, bit_index) * scales[1 + bit_index])
    device_state = jnp.sum(span_states, axis=0)
    scaled_seq = g_half[:, :, None] * level_coef[:, :, 1 + local_bits :, :, None]
    device_terms = split_einsum("jchd,jclhe->lhde", q_half, scaled_seq)
    found_states = lower_blocks(device_state, position, seq_bits)
    gathered = upper_blocks(device_terms, position, seq_bits)
    for bit_index in range(seq_bits):
        level_reads.append(
            split_einsum("jchd,hde->jche", q_half, found_states[bit_index])
            * scales[1 + local_bits + bit_index]
        )
    attention = jnp.zeros(four_shape, jnp.float32)
    for level_index in range(level_count):
        attention = attention + lookup[:, :, level_index, :, None] * level_reads[level_index]
    attn_rows = attention.reshape(tok_rows, heads_here * head_size).astype(jnp.bfloat16)
    partial_value = jnp.dot(attn_rows, out_weight, preferred_element_type=jnp.float32)
    mixed = lax.psum_scatter(
        partial_value.astype(jnp.bfloat16), "head", scatter_dimension=1, tiled=True
    )
    weight_norm = 1.0 / math.sqrt(tok_rows * seq_count)
    out_weight_grad = lax.psum_scatter(
        jnp.einsum("tj,ti->ji", full_rows, attn_rows, preferred_element_type=jnp.float32)
        * weight_norm,
        "seq",
        scatter_dimension=0,
        tiled=True,
    )
    level_grads = jnp.stack(
        [jnp.sum(g_half * level_reads[level_index], axis=3) for level_index in range(level_count)],
        axis=2,
    )
    table_norm = 1.0 / math.sqrt(tok_rows * seq_count * level_count)
    table_part = (
        jnp.einsum(
            "tlc,tlh->ch",
            one_hot,
            level_grads.reshape(tok_rows, level_count, heads_here),
            precision=HIGHEST_PRECISION,
        )
        * table_norm
    )
    table_grad = lax.psum(table_part, "seq")
    within_coef = jnp.transpose(level_coef[:, :, 0, :], (0, 2, 1))[:, :, :, None]
    score_grads = (
        jnp.einsum("jche,jshe->jhcs", g_half, v_half, preferred_element_type=jnp.float32)
        * causal
        * within_coef
    )
    query_grad = split_einsum("jhcs,jshd->jchd", score_grads, k_half)
    key_grad = split_einsum("jhcs,jchd->jshd", score_grads, q_half)
    value_grad = split_einsum("jhcs,jche->jshe", scores * within_coef, g_half)
    upper_terms = jnp.zeros_like(span_states)
    for bit_index in range(local_bits):
        coef_here = level_coef[:, :, 1 + bit_index, :, None]
        query_part = upper_half(coef_here, bit_index) * split_einsum(
            "gjche,ghde->gjchd", upper_half(g_half, bit_index), local_lower[bit_index]
        )
        query_grad = query_grad + place_upper(query_part, bit_index)
        scaled_grads = upper_half(g_half * coef_here, bit_index)
        block_terms = split_einsum("gjchd,gjche->ghde", upper_half(q_half, bit_index), scaled_grads)
        upper_terms = upper_terms + spread_lower(block_terms, bit_index)
    for bit_index in range(seq_bits):
        coef_here = level_coef[:, :, 1 + local_bits + bit_index, :, None]
        query_grad = query_grad + coef_here * split_einsum(
            "jche,hde->jchd", g_half, found_states[bit_index]
        )
    states_back = upper_terms + gathered[None]
    key_grad = key_grad + split_einsum("jhde,jche->jchd", states_back, v_half)
    value_grad = value_grad + split_einsum("jhde,jchd->jche", states_back, k_half)
    flat_shape = (tok_rows, heads_here * head_size)
    return (
        mixed,
        out_weight_grad,
        query_grad.reshape(flat_shape).astype(jnp.bfloat16),
        key_grad.reshape(flat_shape).astype(jnp.bfloat16),
        value_grad.reshape(flat_shape).astype(jnp.bfloat16),
        table_grad,
    )


def solution(mesh):
    placed = (
        P("seq", "head"),
        P("seq", "head"),
        P("seq", "head"),
        P(None, "head"),
        P("seq", None),
        P("head", None),
        P("seq", "head"),
    )
    return jax.shard_map(
        per_device,
        mesh=mesh,
        in_specs=placed,
        out_specs=(
            P("seq", "head"),
            P("seq", "head"),
            P("seq", "head"),
            P("seq", "head"),
            P("seq", "head"),
            P(None, "head"),
        ),
        check_vma=False,
    )
```

profile of v0, /device:TPU:0, one launch (start us, length us, event | category | flops | bytes accessed | tf_op | source)
XLA Modules:
  0.0 191.6 jit_solution(12065787987830475894)
XLA Ops:
  7.2 1.9 reshape.213
  10.1 1.3 fusion.171
  12.8 3.0 %collective-permute-start = (bf16[4,128,128]{2,1,0:T(8,128)(2,1)}, bf16[4,128,128]{2,1,0:T(8,128)(2,1)S(1)}, u32[]{:S(2)}, u32[]{:S(2)}) collective-permute-start(bf16[4,128,128]{2,1,0:T(8,128)(2,1)} %convert_element_type.273), channel_id=1, source_target_pairs={{0,4},{4,0},{8,12},{12,8},{16,20},{20,16},{24,28},{28,24},{1,5},{5... | collective-permute-start | bytes 393224 | tf_op jit(solution)/shard_map/ppermute | solution.py:14
  15.8 1.7 reshape.212
  17.6 1.7 reshape_reshape.14
  19.3 1.7 reshape_reshape.15
  21.0 1.1 slice.122
  25.6 1.3 fusion.128
  26.9 2.0 %fusion.19 = f32[2,1,64,4,128]{4,2,3,1,0:T(8,128)} fusion(f32[2,4,128,64]{2,3,1,0:T(8,128)S(1)} %fusion.128, bf16[2,1,64,4,128]{4,3,2,1,0:T(4,128)(2,1)S(1)} %slice.119, f32[2,2,4,128,128]{4,3,2,1,0:T(8,128)} %bitcast.372), kind=kOutput, calls=%fused_computation.36 | convolution fusion | flops 17367040 | bytes 1179648 | tf_op jit(solution)/shard_map/gjchd,ghde->gjche/dot_general | solution.py:26
  28.9 1.3 convolution_multiply_fusion.1
  30.2 1.1 fusion.109
  32.0 1.4 reshape.215
  33.5 1.8 concatenate.19.clone
  35.2 1.8 fusion.61
  37.0 1.5 broadcast_multiply_fusion
  39.2 1.6 collective-permute-start.1
  42.8 1.4 collective-permute-done.1
  44.2 2.7 %collective-permute-start.2 = (bf16[4,128,128]{2,1,0:T(8,128)(2,1)S(1)}, bf16[4,128,128]{2,1,0:T(8,128)(2,1)S(1)}, u32[]{:S(2)}, u32[]{:S(2)}) collective-permute-start(bf16[4,128,128]{2,1,0:T(8,128)(2,1)S(1)} %fusion.54), channel_id=1, source_target_pairs={{0,16},{4,20},{8,24},{12,28},{16,0},{20,4},{24,8},{28,12},{1,17},{... | collective-permute-start | bytes 393224 | tf_op jit(solution)/shard_map/ppermute | solution.py:14
  48.9 2.9 %collective-permute-done.2 = bf16[4,128,128]{2,1,0:T(8,128)(2,1)S(1)} collective-permute-done((bf16[4,128,128]{2,1,0:T(8,128)(2,1)S(1)}, bf16[4,128,128]{2,1,0:T(8,128)(2,1)S(1)}, u32[]{:S(2)}, u32[]{:S(2)}) %collective-permute-start.2) | collective-permute-done | bytes 131104 | tf_op jit(solution)/shard_map/ppermute | solution.py:14
  51.8 1.0 fusion.80
  53.9 2.0 %convolution_convert_fusion.1 = bf16[256,512]{1,0:T(8,128)(2,1)S(1)} fusion(bf16[256,2048]{1,0:T(8,128)(2,1)} %all-gather.2.cloned.1.call-done, bf16[512,2048]{1,0:T(8,128)(2,1)S(1)} %copy-done), kind=kOutput, calls=%fused_computation.34 | convolution fusion | flops 537001984 | bytes 3407872 | tf_op jit(solution)/shard_map/tj,ij->ti/dot_general | solution.py:108
  55.9 4.5 %fusion.39 = (f32[4,64,4]{1,2,0:T(4,128)}, f32[4,64,4]{1,2,0:T(4,128)}, f32[4,64,4]{1,2,0:T(4,128)}, f32[4,64,4]{1,2,0:T(4,128)}, f32[4,64,4]{1,2,0:T(4,128)}, /...) fusion(f32[4,128,4,64]{1,3,2,0:T(8,128)} %bitcast.385, f32[4,128,4,64]{1,3,2,0:T(8,128)} %bitcast.384, ...), kind=kOutput, calls=%fused_computation.67 | convolution fusion | flops 21620736 | bytes 6078464 | tf_op jit(solution)/shard_map/jhcs,jshe->jche/dot_general | solution.py:21
  60.7 2.7 %multiply_bitcast_fusion = f32[2048,512]{0,1:T(8,128)} fusion(bf16[256,2048]{1,0:T(8,128)(2,1)S(1)} %copy-done.37, bf16[32,8,4,128]{3,2,1,0:T(4,128)(2,1)S(1)} %bitcast.378), kind=kOutput, calls=%fused_computation | convolution fusion | flops 537919488 | bytes 5505024 | tf_op jit(solution)/shard_map/tj,ti->ji/dot_general | solution.py:147
  65.0 1.4 slice_bitcast_fusion.5
  69.7 1.3 copy.248
  71.0 1.4 stack.21
  72.4 1.3 copy.249
  73.7 1.4 stack.22
  75.1 1.3 copy.250
  76.4 1.4 stack.23
  77.7 1.3 copy.251
  79.0 1.4 stack.24
  80.4 1.3 copy.252
  81.7 1.4 stack.25
  83.1 1.3 copy.253
  84.4 1.4 stack.26
  85.7 2.0 %convolution_bitcast_fusion = f32[4,3,128,128]{3,2,1,0:T(8,128)S(1)} fusion(f32[4,64,3,4]{1,0,2,3:T(4,128)} %copy.234, bf16[4,64,4,128,1]{3,2,1,0,4:T(4,128)(2,1)} %bitcast.375, bf16[4,64,4,128]{3,2,1,0:T(4,128)(2,1)S(1)} %reshape.222), kind=kOutput, calls=%fused_computation.5 | convolution fusion | flops 102760448 | bytes 1323008 | tf_op jit(solution)/shard_map/jchd,jclhe->lhde/dot_general | solution.py:26
  87.9 2.1 %fusion.172 = (bf16[3,4,128,128]{2,3,0,1:T(8,128)(2,1)}, f32[3,4,128,128]{2,3,0,1:T(8,128)}) fusion(f32[4,3,128,128]{3,2,1,0:T(8,128)S(1)} %convolution_bitcast_fusion, bf16[4,64,4,128,1]{3,2,1,0,4:T(4,128)(2,1)S(1)} %bitcast.376, f32[4,64,3,4]{1,0,2,3:T(4,128)S(1)} %copy-done.41, bf16[4,64,4,128]{3,2,1,0:T(4,128)(2,1)S(1)} %reshape.222), kind=kOutput, calls=%fused_computation.255 | convolution fusion | flops 101974016 | bytes 2502656 | tf_op jit(solution)/shard_map/jchd,jclhe->lhde/dot_general | solution.py:26
  92.0 1.0 fusion.25
  93.1 1.4 fusion.83
  95.5 1.0 fusion.78
  96.6 1.0 fusion.133
  98.6 1.1 fusion.139
  99.7 1.0 fusion.104
  103.1 1.0 fusion.123
  104.1 1.7 convolution_convert_fusion
  106.0 1.0 concatenate.21.clone
  107.1 3.6 %fusion.16 = bf16[4,64,4,128]{3,1,2,0:T(8,128)(2,1)} fusion(f32[4,64,4,128]{3,1,2,0:T(8,128)S(1)} %bitcast.392, f32[4,4,64,128]{3,2,1,0:T(8,128)} %fusion.123, f32[4,128,4,64]{1,3,2,0:T(8,128)} %bitcast.387, f32[4,128,4,64]{1,3,2,0:T(8,128)} %bitcast.386, f32[4,128,4,64]{1,3,2,0:T(8,128)} %bitcast.389, f32[4,128,4,64]{1,3,2,0:T(8,128)} %bitcast.388, ...), kind=kOutput, calls=%fused_computation.31 | convolution fusion | flops 18743296 | bytes 5255168 | tf_op jit(solution)/shard_map/jhcs,jshd->jchd/dot_general | solution.py:21
  110.6 1.1 convert_element_type.313
  112.7 1.0 fusion.170
  113.9 1.3 fusion.3
  115.3 2.1 %copy.275 = f32[2,1,4,128,128]{4,3,2,1,0:T(8,128)} copy(f32[2,1,4,128,128]{3,4,2,0,1:T(8,128)} %fusion.3) | data formatting | bytes 1048576
  117.4 2.1 %concatenate.23.clone = f32[2,2,4,128,128]{4,3,2,1,0:T(8,128)} pad(f32[2,1,4,128,128]{4,3,2,1,0:T(8,128)} %copy.275, f32[]{:T(128)} %constant.16.clone.1), padding=0_0x0_1x0_0x0_0x0_0 | pad | bytes 1572868 | tf_op jit(solution)/shard_map/concatenate | solution.py:54
  119.5 1.8 copy.231
  121.3 1.2 copy.221
  123.2 21.9 %psum.7 = f32[16,4]{0,1:T(4,128)} all-reduce(f32[16,4]{0,1:T(4,128)S(1)} %fusion.26), channel_id=1, replica_groups=mesh['seq'=8,'head'=4] {'seq'}, use_global_device_ids=true, to_apply=%region_10.0 | all-reduce | flops 64 | bytes 512 | tf_op jit(solution)/shard_map/psum | solution.py:167
  145.1 2.3 %fusion.47 = f32[4,4,128,64]{2,3,1,0:T(8,128)} fusion(f32[4,4,64,64]{3,2,1,0:T(8,128)S(1)} %convolution_multiply_fusion.1, f32[4,4,64]{2,1,0:T(4,128)S(1)} %get-tuple-element.41, bf16[4,64,4,128]{3,2,1,0:T(4,128)(2,1)} %copy-done.3), kind=kOutput, calls=%fused_computation.101 | convolution fusion | flops 16908288 | bytes 1052672 | tf_op jit(solution)/shard_map/jhcs,jche->jshe/dot_general | solution.py:21
  148.5 1.1 fusion.72
  149.6 7.5 %collective-permute-done.5 = bf16[1,4,128,128]{2,3,0,1:T(8,128)(2,1)S(1)} collective-permute-done((bf16[1,4,128,128]{2,3,0,1:T(8,128)(2,1)S(1)}, bf16[1,4,128,128]{2,3,0,1:T(8,128)(2,1)S(1)}, u32[]{:S(2)}, u32[]{:S(2)}) %collective-permute-start.5) | collective-permute-done | bytes 131104 | tf_op jit(solution)/shard_map/ppermute | solution.py:14
  157.1 1.7 fusion.60
  158.9 1.8 copy.237
  161.7 1.6 subtract_convert_fusion
  167.4 2.1 %copy.254 = f32[256,512]{1,0:T(8,128)} copy(f32[256,512]{0,1:T(8,128)} %reduce-scatter.5.cloned.1.call-done) | data formatting | bytes 1048576
  169.5 15.6 %reduce-scatter.3.cloned.1.call-done = bf16[256,512]{1,0:T(8,128)(2,1)} async-done(((bf16[256,2048]{1,0:T(8,128)(2,1)}), bf16[256,512]{1,0:T(8,128)(2,1)}) %reduce-scatter.3.cloned.1.call-update) | async-done | bytes 262160 | tf_op jit(solution)/shard_map/reduce_scatter | solution.py:142
  (195 shorter events, 32.2 us)
Async XLA Ops:
  7.2 46.7 %copy-start = (bf16[512,2048]{1,0:T(8,128)(2,1)S(1)}, bf16[512,2048]{1,0:T(8,128)(2,1)}, u32[]{:S(2)}) copy-start(bf16[512,2048]{1,0:T(8,128)(2,1)} %param.13) | copy-start | bytes 6291460
  7.2 46.7 %all-gather.2.cloned.1.call-start = ((), (), s32[]{:S(2)}) async-start(), calls=%async_computation.3 | async-start | bytes 1310720 | tf_op jit(solution)/shard_map/all_gather | solution.py:107
  11.4 11.6 %copy-start.1 = (f32[4,4,128,128]{3,2,1,0:T(8,128)}, f32[4,4,128,128]{3,2,1,0:T(8,128)S(1)}, u32[]{:S(2)}) copy-start(f32[4,4,128,128]{3,2,1,0:T(8,128)S(1)} %get-tuple-element.51) | copy-start | bytes 3145732
  12.8 26.3 %collective-permute-start = (bf16[4,128,128]{2,1,0:T(8,128)(2,1)}, bf16[4,128,128]{2,1,0:T(8,128)(2,1)S(1)}, u32[]{:S(2)}, u32[]{:S(2)}) collective-permute-start(bf16[4,128,128]{2,1,0:T(8,128)(2,1)} %convert_element_type.273), channel_id=1, source_target_pairs={{0,4},{4,0},{8,12},{12,8},{16,20},{20,16},{24,28},{28,24},{1,5},{5... | collective-permute-start | bytes 393224 | tf_op jit(solution)/shard_map/ppermute | solution.py:14
  15.8 151.6 %reduce-scatter.5.cloned.1.call-start = ((), (), s32[]{:S(2)}) async-start(), calls=%async_computation.4 | async-start | bytes 4718592 | tf_op jit(solution)/shard_map/reduce_scatter | solution.py:146
  21.0 3.5 %copy-start.8 = (bf16[4,64,4,128]{3,2,1,0:T(4,128)(2,1)S(1)}, bf16[4,64,4,128]{3,2,1,0:T(4,128)(2,1)}, u32[]{:S(2)}) copy-start(bf16[4,64,4,128]{3,2,1,0:T(4,128)(2,1)} %reshape.212) | copy-start | bytes 786436
  21.0 2.9 %copy-start.12 = (f32[4,128,128]{2,1,0:T(8,128)}, f32[4,128,128]{2,1,0:T(8,128)S(1)}, u32[]{:S(2)}) copy-start(f32[4,128,128]{2,1,0:T(8,128)S(1)} %slice_reduce_fusion) | copy-start | bytes 786436
  22.1 2.4 %copy-start.35 = (bf16[1,2,64,4,128]{4,3,2,1,0:T(4,128)(2,1)}, bf16[1,2,64,4,128]{4,3,2,1,0:T(4,128)(2,1)S(1)}, u32[]{:S(2)}) copy-start(bf16[1,2,64,4,128]{4,3,2,1,0:T(4,128)(2,1)S(1)} %slice.122) | copy-start | bytes 393220
  25.6 3.3 %copy-start.18 = (bf16[2,1,64,4,128]{4,3,2,1,0:T(4,128)(2,1)}, bf16[2,1,64,4,128]{4,3,2,1,0:T(4,128)(2,1)S(1)}, u32[]{:S(2)}) copy-start(bf16[2,1,64,4,128]{4,3,2,1,0:T(4,128)(2,1)S(1)} %slice.119) | copy-start | bytes 393220
  25.6 5.7 %copy-start.54 = (s32[256,6]{0,1:T(8,128)S(1)}, s32[256,6]{0,1:T(8,128)}, u32[]{:S(2)}) copy-start(s32[256,6]{0,1:T(8,128)} %param.12) | copy-start | bytes 18436
  25.6 5.7 %copy-start.56 = (f32[16,4]{0,1:T(4,128)S(1)}, f32[16,4]{0,1:T(4,128)}, u32[]{:S(2)}) copy-start(f32[16,4]{0,1:T(4,128)} %param.11) | copy-start | bytes 772
  28.9 8.2 %copy-start.59 = (f32[6]{0:T(128)S(1)}, f32[6]{0:T(128)}, u32[]{:S(2)}) copy-start(f32[6]{0:T(128)} %constant.13.clone) | copy-start | bytes 76
  28.9 10.3 %copy-start.15 = (f32[4,128,128]{2,1,0:T(8,128)S(1)}, f32[4,128,128]{2,1,0:T(8,128)}, u32[]{:S(2)}) copy-start(f32[4,128,128]{2,1,0:T(8,128)} %copy-done.14) | copy-start | bytes 786436
  39.2 5.0 %collective-permute-start.1 = (bf16[4,128,128]{2,1,0:T(8,128)(2,1)S(1)}, bf16[4,128,128]{2,1,0:T(8,128)(2,1)S(1)}, u32[]{:S(2)}, u32[]{:S(2)}) collective-permute-start(bf16[4,128,128]{2,1,0:T(8,128)(2,1)S(1)} %fusion.77), channel_id=1, source_target_pairs={{0,8},{4,12},{8,0},{12,4},{16,24},{20,28},{24,16},{28,20},{1,9},{5... | collective-permute-start | bytes 393224 | tf_op jit(solution)/shard_map/ppermute | solution.py:14
  44.2 3.7 %copy-start.16 = (bf16[4,128,128]{2,1,0:T(8,128)(2,1)}, bf16[4,128,128]{2,1,0:T(8,128)(2,1)S(1)}, u32[]{:S(2)}) copy-start(bf16[4,128,128]{2,1,0:T(8,128)(2,1)S(1)} %collective-permute-done.1) | copy-start | bytes 393220
  44.2 7.6 %collective-permute-start.2 = (bf16[4,128,128]{2,1,0:T(8,128)(2,1)S(1)}, bf16[4,128,128]{2,1,0:T(8,128)(2,1)S(1)}, u32[]{:S(2)}, u32[]{:S(2)}) collective-permute-start(bf16[4,128,128]{2,1,0:T(8,128)(2,1)S(1)} %fusion.54), channel_id=1, source_target_pairs={{0,16},{4,20},{8,24},{12,28},{16,0},{20,4},{24,8},{28,12},{1,17},{... | collective-permute-start | bytes 393224 | tf_op jit(solution)/shard_map/ppermute | solution.py:14
  51.8 2.0 %copy-start.29 = (bf16[4,128,128]{2,1,0:T(8,128)(2,1)}, bf16[4,128,128]{2,1,0:T(8,128)(2,1)S(1)}, u32[]{:S(2)}) copy-start(bf16[4,128,128]{2,1,0:T(8,128)(2,1)S(1)} %collective-permute-done.2) | copy-start | bytes 393220
  55.8 4.6 %copy-start.26 = (bf16[256,512]{1,0:T(8,128)(2,1)}, bf16[256,512]{1,0:T(8,128)(2,1)S(1)}, u32[]{:S(2)}) copy-start(bf16[256,512]{1,0:T(8,128)(2,1)S(1)} %convolution_convert_fusion.1) | copy-start | bytes 786436
  55.9 31.9 %copy-start.3 = (bf16[4,64,4,128]{3,2,1,0:T(4,128)(2,1)}, bf16[4,64,4,128]{3,2,1,0:T(4,128)(2,1)S(1)}, u32[]{:S(2)}) copy-start(bf16[4,64,4,128]{3,2,1,0:T(4,128)(2,1)S(1)} %reshape.222) | copy-start | bytes 786436
  55.9 4.7 %copy-start.37 = (bf16[256,2048]{1,0:T(8,128)(2,1)S(1)}, bf16[256,2048]{1,0:T(8,128)(2,1)}, u32[]{:S(2)}) copy-start(bf16[256,2048]{1,0:T(8,128)(2,1)} %all-gather.2.cloned.1.call-done) | copy-start | bytes 3145732
  60.6 2.7 %copy-start.23 = (bf16[4,64,4,128]{3,2,1,0:T(4,128)(2,1)}, bf16[4,64,4,128]{3,2,1,0:T(4,128)(2,1)S(1)}, u32[]{:S(2)}) copy-start(bf16[4,64,4,128]{3,2,1,0:T(4,128)(2,1)S(1)} %copy.197) | copy-start | bytes 786436
  63.4 4.8 %copy-start.27 = (bf16[256,512]{1,0:T(8,128)(2,1)S(1)}, bf16[256,512]{1,0:T(8,128)(2,1)}, u32[]{:S(2)}) copy-start(bf16[256,512]{1,0:T(8,128)(2,1)} %copy-done.26) | copy-start | bytes 786436
  63.4 121.6 %reduce-scatter.3.cloned.1.call-start = ((), (), s32[]{:S(2)}) async-start(), calls=%async_computation.2 | async-start | bytes 1310720 | tf_op jit(solution)/shard_map/reduce_scatter | solution.py:142
  85.7 2.1 %copy-start.9 = (bf16[4,64,4,128]{3,2,1,0:T(4,128)(2,1)S(1)}, bf16[4,64,4,128]{3,2,1,0:T(4,128)(2,1)}, u32[]{:S(2)}) copy-start(bf16[4,64,4,128]{3,2,1,0:T(4,128)(2,1)} %reshape.212) | copy-start | bytes 786436
  85.7 2.1 %copy-start.41 = (f32[4,64,3,4]{1,0,2,3:T(4,128)S(1)}, f32[4,64,3,4]{1,0,2,3:T(4,128)}, u32[]{:S(2)}) copy-start(f32[4,64,3,4]{1,0,2,3:T(4,128)} %copy.234) | copy-start | bytes 36868
  85.7 5.2 %copy-start.39 = (bf16[2,2,64,4,128]{4,3,2,1,0:T(4,128)(2,1)S(1)}, bf16[2,2,64,4,128]{4,3,2,1,0:T(4,128)(2,1)}, u32[]{:S(2)}) copy-start(bf16[2,2,64,4,128]{4,3,2,1,0:T(4,128)(2,1)} %reshape_reshape.16) | copy-start | bytes 786436
  85.7 5.2 %copy-start.38 = (bf16[1,4,64,4,128]{4,3,2,1,0:T(4,128)(2,1)S(1)}, bf16[1,4,64,4,128]{4,3,2,1,0:T(4,128)(2,1)}, u32[]{:S(2)}) copy-start(bf16[1,4,64,4,128]{4,3,2,1,0:T(4,128)(2,1)} %reshape_reshape.17) | copy-start | bytes 786436
  87.8 3.3 %copy-start.48 = (f32[256,1,4]{0,2,1:T(4,128)S(1)}, f32[256,1,4]{0,2,1:T(4,128)}, u32[]{:S(2)}) copy-start(f32[256,1,4]{0,2,1:T(4,128)} %stack.21) | copy-start | bytes 12292
  87.8 3.3 %copy-start.49 = (f32[256,1,4]{0,2,1:T(4,128)S(1)}, f32[256,1,4]{0,2,1:T(4,128)}, u32[]{:S(2)}) copy-start(f32[256,1,4]{0,2,1:T(4,128)} %stack.22) | copy-start | bytes 12292
  87.8 3.3 %copy-start.50 = (f32[256,1,4]{0,2,1:T(4,128)S(1)}, f32[256,1,4]{0,2,1:T(4,128)}, u32[]{:S(2)}) copy-start(f32[256,1,4]{0,2,1:T(4,128)} %stack.23) | copy-start | bytes 12292
  87.8 3.3 %copy-start.51 = (f32[256,1,4]{0,2,1:T(4,128)S(1)}, f32[256,1,4]{0,2,1:T(4,128)}, u32[]{:S(2)}) copy-start(f32[256,1,4]{0,2,1:T(4,128)} %stack.24) | copy-start | bytes 12292
  87.9 3.3 %copy-start.52 = (f32[256,1,4]{0,2,1:T(4,128)S(1)}, f32[256,1,4]{0,2,1:T(4,128)}, u32[]{:S(2)}) copy-start(f32[256,1,4]{0,2,1:T(4,128)} %stack.25) | copy-start | bytes 12292
  87.9 3.3 %copy-start.53 = (f32[256,1,4]{0,2,1:T(4,128)S(1)}, f32[256,1,4]{0,2,1:T(4,128)}, u32[]{:S(2)}) copy-start(f32[256,1,4]{0,2,1:T(4,128)} %stack.26) | copy-start | bytes 12292
  87.9 3.3 %copy-start.36 = (bf16[1,2,64,4,128]{4,3,2,1,0:T(4,128)(2,1)S(1)}, bf16[1,2,64,4,128]{4,3,2,1,0:T(4,128)(2,1)}, u32[]{:S(2)}) copy-start(bf16[1,2,64,4,128]{4,3,2,1,0:T(4,128)(2,1)} %copy-done.35) | copy-start | bytes 393220
  87.9 3.3 %copy-start.47 = (f32[2,64,4]{1,0,2:T(2,128)S(1)}, f32[2,64,4]{1,0,2:T(2,128)}, u32[]{:S(2)}) copy-start(f32[2,64,4]{1,0,2:T(2,128)} %copy.430) | copy-start | bytes 6148
  87.9 3.7 %copy-start.13 = (f32[4,128,128]{2,1,0:T(8,128)S(1)}, f32[4,128,128]{2,1,0:T(8,128)}, u32[]{:S(2)}) copy-start(f32[4,128,128]{2,1,0:T(8,128)} %copy-done.12) | copy-start | bytes 786436
  90.0 3.1 %copy-start.19 = (bf16[2,1,64,4,128]{4,3,2,1,0:T(4,128)(2,1)S(1)}, bf16[2,1,64,4,128]{4,3,2,1,0:T(4,128)(2,1)}, u32[]{:S(2)}) copy-start(bf16[2,1,64,4,128]{4,3,2,1,0:T(4,128)(2,1)} %copy-done.18) | copy-start | bytes 393220
  90.0 4.4 %copy-start.46 = (f32[2,64,4]{1,2,0:T(4,128)S(1)}, f32[2,64,4]{1,2,0:T(4,128)}, u32[]{:S(2)}) copy-start(f32[2,64,4]{1,2,0:T(4,128)} %slice_bitcast_fusion.7) | copy-start | bytes 6148
  90.0 20.6 %collective-permute-start.3 = (bf16[3,4,128,128]{2,3,0,1:T(8,128)(2,1)}, bf16[3,4,128,128]{2,3,0,1:T(8,128)(2,1)}, u32[]{:S(2)}, u32[]{:S(2)}) collective-permute-start(bf16[3,4,128,128]{2,3,0,1:T(8,128)(2,1)} %get-tuple-element.52), channel_id=1, source_target_pairs={{0,4},{4,0},{8,12},{12,8},{16,20},{20,16},{24,28},{28,24},{1,5},{5... | collective-permute-start | bytes 1179656 | tf_op jit(solution)/shard_map/ppermute | solution.py:14
  91.0 11.1 %copy-start.21 = (bf16[2,1,64,4,128]{4,3,2,1,0:T(4,128)(2,1)}, bf16[2,1,64,4,128]{4,3,2,1,0:T(4,128)(2,1)S(1)}, u32[]{:S(2)}) copy-start(bf16[2,1,64,4,128]{4,3,2,1,0:T(4,128)(2,1)S(1)} %slice.131) | copy-start | bytes 393220
  91.2 4.0 %copy-start.57 = (f32[256,6,4]{0,2,1:T(4,128)}, f32[256,6,4]{0,2,1:T(4,128)S(1)}, u32[]{:S(2)}) copy-start(f32[256,6,4]{0,2,1:T(4,128)S(1)} %constant_dynamic-update-slice_fusion) | copy-start | bytes 73732
  91.2 4.0 %copy-start.2 = (f32[4,4,128,128]{3,2,1,0:T(8,128)S(1)}, f32[4,4,128,128]{3,2,1,0:T(8,128)}, u32[]{:S(2)}) copy-start(f32[4,4,128,128]{3,2,1,0:T(8,128)} %copy-done.1) | copy-start | bytes 3145732
  91.8 3.7 %copy-start.30 = (bf16[4,128,128]{2,1,0:T(8,128)(2,1)S(1)}, bf16[4,128,128]{2,1,0:T(8,128)(2,1)}, u32[]{:S(2)}) copy-start(bf16[4,128,128]{2,1,0:T(8,128)(2,1)} %copy-done.29) | copy-start | bytes 393220
  93.1 4.6 %copy-start.17 = (bf16[4,128,128]{2,1,0:T(8,128)(2,1)S(1)}, bf16[4,128,128]{2,1,0:T(8,128)(2,1)}, u32[]{:S(2)}) copy-start(bf16[4,128,128]{2,1,0:T(8,128)(2,1)} %copy-done.16) | copy-start | bytes 393220
  96.6 5.2 %copy-start.4 = (bf16[4,64,4,128]{3,2,1,0:T(4,128)(2,1)S(1)}, bf16[4,64,4,128]{3,2,1,0:T(4,128)(2,1)}, u32[]{:S(2)}) copy-start(bf16[4,64,4,128]{3,2,1,0:T(4,128)(2,1)} %copy-done.3) | copy-start | bytes 786436
  96.6 5.2 %copy-start.40 = (f32[64,64]{1,0:T(8,128)S(1)}, f32[64,64]{1,0:T(8,128)}, u32[]{:S(2)}) copy-start(f32[64,64]{1,0:T(8,128)} %fusion.145) | copy-start | bytes 49156
  98.6 3.4 %copy-start.45 = (f32[2,64,4]{1,2,0:T(4,128)S(1)}, f32[2,64,4]{1,2,0:T(4,128)}, u32[]{:S(2)}) copy-start(f32[2,64,4]{1,2,0:T(4,128)} %slice_bitcast_fusion.8) | copy-start | bytes 6148
  99.7 3.4 %copy-start.6 = (bf16[4,64,4,128]{3,2,1,0:T(4,128)(2,1)S(1)}, bf16[4,64,4,128]{3,2,1,0:T(4,128)(2,1)}, u32[]{:S(2)}) copy-start(bf16[4,64,4,128]{3,2,1,0:T(4,128)(2,1)} %reshape.213) | copy-start | bytes 786436
  100.8 3.3 %copy-start.24 = (bf16[4,64,4,128]{3,2,1,0:T(4,128)(2,1)S(1)}, bf16[4,64,4,128]{3,2,1,0:T(4,128)(2,1)}, u32[]{:S(2)}) copy-start(bf16[4,64,4,128]{3,2,1,0:T(4,128)(2,1)} %copy-done.23) | copy-start | bytes 786436
  103.1 2.8 %copy-start.55 = (s32[256,6]{0,1:T(8,128)S(1)}, s32[256,6]{0,1:T(8,128)}, u32[]{:S(2)}) copy-start(s32[256,6]{0,1:T(8,128)} %param.12) | copy-start | bytes 18436
  103.1 2.8 %copy-start.58 = (f32[256,6,4]{0,2,1:T(4,128)S(1)}, f32[256,6,4]{0,2,1:T(4,128)}, u32[]{:S(2)}) copy-start(f32[256,6,4]{0,2,1:T(4,128)} %copy-done.57) | copy-start | bytes 73732
  104.1 2.9 %copy-start.42 = (f32[4,64,4]{1,2,0:T(4,128)S(1)}, f32[4,64,4]{1,2,0:T(4,128)}, u32[]{:S(2)}) copy-start(f32[4,64,4]{1,2,0:T(4,128)} %get-tuple-element.36) | copy-start | bytes 12292
  104.1 2.9 %copy-start.43 = (f32[4,64,4]{1,2,0:T(4,128)S(1)}, f32[4,64,4]{1,2,0:T(4,128)}, u32[]{:S(2)}) copy-start(f32[4,64,4]{1,2,0:T(4,128)} %get-tuple-element.37) | copy-start | bytes 12292
  104.1 2.9 %copy-start.44 = (f32[4,64,4]{1,2,0:T(4,128)S(1)}, f32[4,64,4]{1,2,0:T(4,128)}, u32[]{:S(2)}) copy-start(f32[4,64,4]{1,2,0:T(4,128)} %get-tuple-element.38) | copy-start | bytes 12292
  107.1 5.6 %copy-start.28 = (f32[3,4,128,128]{2,3,0,1:T(8,128)S(1)}, f32[3,4,128,128]{2,3,0,1:T(8,128)}, u32[]{:S(2)}) copy-start(f32[3,4,128,128]{2,3,0,1:T(8,128)} %get-tuple-element.53) | copy-start | bytes 2359300
  110.6 3.3 %copy-start.20 = (bf16[2,1,64,4,128]{4,3,2,1,0:T(4,128)(2,1)S(1)}, bf16[2,1,64,4,128]{4,3,2,1,0:T(4,128)(2,1)}, u32[]{:S(2)}) copy-start(bf16[2,1,64,4,128]{4,3,2,1,0:T(4,128)(2,1)} %copy-done.18) | copy-start | bytes 393220
  110.6 3.3 %copy-start.22 = (bf16[2,1,64,4,128]{4,3,2,1,0:T(4,128)(2,1)S(1)}, bf16[2,1,64,4,128]{4,3,2,1,0:T(4,128)(2,1)}, u32[]{:S(2)}) copy-start(bf16[2,1,64,4,128]{4,3,2,1,0:T(4,128)(2,1)} %copy-done.21) | copy-start | bytes 393220
  110.6 3.3 %copy-start.31 = (f32[2,4,128,128]{3,2,1,0:T(8,128)S(1)}, f32[2,4,128,128]{3,2,1,0:T(8,128)}, u32[]{:S(2)}) copy-start(f32[2,4,128,128]{3,2,1,0:T(8,128)} %fusion.83) | copy-start | bytes 1572868
  113.7 33.7 %collective-permute-start.4 = (bf16[2,4,128,128]{2,3,0,1:T(8,128)(2,1)}, bf16[2,4,128,128]{2,3,0,1:T(8,128)(2,1)}, u32[]{:S(2)}, u32[]{:S(2)}) collective-permute-start(bf16[2,4,128,128]{2,3,0,1:T(8,128)(2,1)} %get-tuple-element.30), channel_id=1, source_target_pairs={{0,8},{4,12},{8,0},{12,4},{16,24},{20,28},{24,16},{28,20},{1,9},{5... | collective-permute-start | bytes 786440 | tf_op jit(solution)/shard_map/ppermute | solution.py:14
  145.1 3.3 %copy-start.34 = (f32[2,4,128,128]{2,3,0,1:T(8,128)S(1)}, f32[2,4,128,128]{2,3,0,1:T(8,128)}, u32[]{:S(2)}) copy-start(f32[2,4,128,128]{2,3,0,1:T(8,128)} %get-tuple-element.31) | copy-start | bytes 1572868
  145.1 3.4 %copy-start.10 = (bf16[4,64,4,128]{3,2,1,0:T(4,128)(2,1)S(1)}, bf16[4,64,4,128]{3,2,1,0:T(4,128)(2,1)}, u32[]{:S(2)}) copy-start(bf16[4,64,4,128]{3,2,1,0:T(4,128)(2,1)} %reshape.212) | copy-start | bytes 786436
  148.4 8.7 %collective-permute-start.5 = (bf16[1,4,128,128]{2,3,0,1:T(8,128)(2,1)S(1)}, bf16[1,4,128,128]{2,3,0,1:T(8,128)(2,1)S(1)}, u32[]{:S(2)}, u32[]{:S(2)}) collective-permute-start(bf16[1,4,128,128]{2,3,0,1:T(8,128)(2,1)S(1)} %fusion.57), channel_id=1, source_target_pairs={{0,16},{4,20},{8,24},{12,28},{16,0},{20,4},{24,8},{28,12},{1,17},{... | collective-permute-start | bytes 393224 | tf_op jit(solution)/shard_map/ppermute | solution.py:14
  163.7 1.2 copy-start.7
  164.6 1.2 copy-start.32
  (5 other events, 4.6 us)
Sparse Core Ops, SparseCore 0:
  15.9 17.0 all-gather.1
  63.5 93.6 reduce-scatter.4
  160.3 24.6 reduce-scatter.2
where the time goes:
time: 193 us; the launch traced here: 192 us
  local copies, waits for them, and re-layouts  53.3 us (28%)
  matrix products  53.1 us (28%)
  waiting for transfers between devices  27.4 us (14%)
  blocking collectives  21.9 us (11%)
  between operations  14.5 us (8%)
  other arithmetic  12.5 us (6%)
  starting transfers between devices  8.79 us (5%)
    psum x1, blocking collectives, per_device(): table_grad = lax.psum(table_part, 'seq')  21.9 us
    reduce_scatter x1, waiting for transfers between devices, per_device(): lax.psum_scatter(partial_value.astype(jnp.bfloat16), 'head', scatter_dime...  15.6 us
    unnamed x16, matrix products  14.5 us
    ppermute x6, waiting for transfers between devices, partner_2(): return lax.ppermute(value, axis, pairs)  11.8 us
    dot_general x6, matrix products, split_einsum(): jnp.einsum(form, rest, right, preferred_element_type=jnp.float32)  9.52 us
    ppermute x6, starting transfers between devices, partner_2(): return lax.ppermute(value, axis, pairs)  8.49 us
    another operation x7, local copies, waits for them, and re-layouts, per_device(): jnp.stack([jnp.sum(g_half * level_reads[level_index], axis=3) for level_i...  8.22 us
    unnamed x131, local copies, waits for them, and re-layouts  7.97 us
  transfers between devices with their start and end apart: 9, of which 4 were waited for; matrix products, arithmetic and copies ran while one was open for 53% of the time, Pallas kernels for 0%

commit v1 on v0

--- a/solution.py
+++ b/solution.py
@@ -164,7 +164,7 @@
         )
         * table_norm
     )
-    table_grad = lax.psum(table_part, "seq")
+    table_grad = jnp.sum(lax.all_gather(table_part, "seq"), axis=0)
     within_coef = jnp.transpose(level_coef[:, :, 0, :], (0, 2, 1))[:, :, :, None]
     score_grads = (
         jnp.einsum("jche,jshe->jhcs", g_half, v_half, preferred_element_type=jnp.float32)

time: 193 us -> 186 us (0.964)
  waiting for transfers between devices: 27.4 us -> 17.3 us
  blocking collectives: 21.9 us -> 28.4 us
  local copies, waits for them, and re-layouts: 53.3 us -> 48.4 us
    all_gather x0 -> x1, blocking collectives: none -> 28.4 us  [per_device(): table_grad = jnp.sum(lax.all_gather(table_part, 'seq'), axis=0)]
    psum x1 -> x0, blocking collectives: 21.9 us -> none  [per_device(): table_grad = lax.psum(table_part, 'seq')]
    reduce_scatter x1, waiting for transfers between devices: 15.6 us -> 7.36 us  [per_device(): lax.psum_scatter(partial_value.astype(jnp.bfloat16), 'head', scatter_dime...]
    unnamed x131 -> x125, local copies, waits for them, and re-layouts: 7.97 us -> 7.19 us
  transfers between devices with their start and end apart: 9 -> 9, of which waited for: 4 -> 4; matrix products, arithmetic and copies ran while one was open for 53% -> 54% of each run, Pallas kernels for 0% -> 0%
where the time goes in v1:
time: 186 us; the launch traced here: 184 us
  matrix products  52.5 us (28%)
  local copies, waits for them, and re-layouts  48.4 us (26%)
  blocking collectives  28.4 us (15%)
  waiting for transfers between devices  17.3 us (9%)
  between operations  14.5 us (8%)
  other arithmetic  14.2 us (8%)
  starting transfers between devices  8.85 us (5%)
    all_gather x1, blocking collectives, per_device(): table_grad = jnp.sum(lax.all_gather(table_part, 'seq'), axis=0)  28.4 us
    unnamed x16, matrix products  14.6 us
    ppermute x6, waiting for transfers between devices, partner_2(): return lax.ppermute(value, axis, pairs)  9.88 us
    dot_general x6, matrix products, split_einsum(): jnp.einsum(form, rest, right, preferred_element_type=jnp.float32)  9.54 us
    ppermute x6, starting transfers between devices, partner_2(): return lax.ppermute(value, axis, pairs)  8.55 us
    another operation x7, local copies, waits for them, and re-layouts, per_device(): jnp.stack([jnp.sum(g_half * level_reads[level_index], axis=3) for level_i...  8.21 us
    reduce_sum x6, local copies, waits for them, and re-layouts, per_device(): jnp.sum(g_half * level_reads[level_index], axis=3)  7.77 us
    reduce_scatter x1, waiting for transfers between devices, per_device(): lax.psum_scatter(partial_value.astype(jnp.bfloat16), 'head', scatter_dime...  7.36 us
  transfers between devices with their start and end apart: 9, of which 4 were waited for; matrix products, arithmetic and copies ran while one was open for 54% of the time, Pallas kernels for 0%

profile of v1, /device:TPU:0, one launch (start us, length us, event | category | flops | bytes accessed | tf_op | source)
XLA Modules:
  0.0 184.2 jit_solution(5064678429881116011)
XLA Ops:
  7.2 1.2 reshape.213
  8.4 1.1 reshape.214
  9.6 1.4 fusion.172
  11.6 3.0 %collective-permute-start = (bf16[4,128,128]{2,1,0:T(8,128)(2,1)}, bf16[4,128,128]{2,1,0:T(8,128)(2,1)S(1)}, u32[]{:S(2)}, u32[]{:S(2)}) collective-permute-start(bf16[4,128,128]{2,1,0:T(8,128)(2,1)} %convert_element_type.273), channel_id=1, source_target_pairs={{0,4},{4,0},{8,12},{12,8},{16,20},{20,16},{24,28},{28,24},{1,5},{5... | collective-permute-start | bytes 393224 | tf_op jit(solution)/shard_map/ppermute | solution.py:14
  16.3 1.1 slice_reduce_fusion
  17.4 1.0 slice.122
  22.0 1.4 fusion.129
  23.4 2.0 %fusion.19 = f32[2,1,64,4,128]{4,2,3,1,0:T(8,128)} fusion(f32[2,4,128,64]{2,3,1,0:T(8,128)S(1)} %fusion.129, bf16[2,1,64,4,128]{4,3,2,1,0:T(4,128)(2,1)S(1)} %slice.119, f32[2,2,4,128,128]{4,3,2,1,0:T(8,128)} %bitcast.376), kind=kOutput, calls=%fused_computation.36 | convolution fusion | flops 17367040 | bytes 1179648 | tf_op jit(solution)/shard_map/gjchd,ghde->gjche/dot_general | solution.py:26
  25.4 1.2 convolution_multiply_fusion.1
  26.6 1.0 fusion.110
  28.4 1.4 reshape.215
  29.9 1.8 concatenate.19.clone
  31.7 1.8 fusion.62
  33.5 1.5 broadcast_multiply_fusion
  35.6 1.5 collective-permute-start.1
  38.1 1.0 fusion.138
  39.2 1.5 collective-permute-done.1
  40.7 2.6 %collective-permute-start.2 = (bf16[4,128,128]{2,1,0:T(8,128)(2,1)S(1)}, bf16[4,128,128]{2,1,0:T(8,128)(2,1)S(1)}, u32[]{:S(2)}, u32[]{:S(2)}) collective-permute-start(bf16[4,128,128]{2,1,0:T(8,128)(2,1)S(1)} %fusion.55), channel_id=1, source_target_pairs={{0,16},{4,20},{8,24},{12,28},{16,0},{20,4},{24,8},{28,12},{1,17},{... | collective-permute-start | bytes 393224 | tf_op jit(solution)/shard_map/ppermute | solution.py:14
  43.3 1.0 fusion.103
  44.3 1.0 fusion.142
  45.3 2.8 %collective-permute-done.2 = bf16[4,128,128]{2,1,0:T(8,128)(2,1)S(1)} collective-permute-done((bf16[4,128,128]{2,1,0:T(8,128)(2,1)S(1)}, bf16[4,128,128]{2,1,0:T(8,128)(2,1)S(1)}, u32[]{:S(2)}, u32[]{:S(2)}) %collective-permute-start.2) | collective-permute-done | bytes 131104 | tf_op jit(solution)/shard_map/ppermute | solution.py:14
  48.2 1.0 fusion.81
  50.2 2.0 %convolution_convert_fusion.1 = bf16[256,512]{1,0:T(8,128)(2,1)S(1)} fusion(bf16[256,2048]{1,0:T(8,128)(2,1)} %all-gather.4.cloned.1.call-done, bf16[512,2048]{1,0:T(8,128)(2,1)S(1)} %copy-done), kind=kOutput, calls=%fused_computation.34 | convolution fusion | flops 537001984 | bytes 3407872 | tf_op jit(solution)/shard_map/tj,ij->ti/dot_general | solution.py:108
  52.3 4.5 %fusion.40 = (f32[4,64,4]{1,2,0:T(4,128)}, f32[4,64,4]{1,2,0:T(4,128)}, f32[4,64,4]{1,2,0:T(4,128)}, f32[4,64,4]{1,2,0:T(4,128)}, f32[4,64,4]{1,2,0:T(4,128)}, /...) fusion(f32[4,128,4,64]{1,3,2,0:T(8,128)} %bitcast.389, f32[4,128,4,64]{1,3,2,0:T(8,128)} %bitcast.388, ...), kind=kOutput, calls=%fused_computation.68 | convolution fusion | flops 21620736 | bytes 6078464 | tf_op jit(solution)/shard_map/jhcs,jshe->jche/dot_general | solution.py:21
  57.1 2.7 %multiply_bitcast_fusion = f32[2048,512]{0,1:T(8,128)} fusion(bf16[256,2048]{1,0:T(8,128)(2,1)S(1)} %copy-done.34, bf16[32,8,4,128]{3,2,1,0:T(4,128)(2,1)S(1)} %bitcast.382), kind=kOutput, calls=%fused_computation | convolution fusion | flops 537919488 | bytes 5505024 | tf_op jit(solution)/shard_map/tj,ti->ji/dot_general | solution.py:147
  61.4 1.4 slice_bitcast_fusion.5
  66.1 1.3 copy.248
  67.4 1.4 stack.21
  68.8 1.3 copy.249
  70.1 1.4 stack.22
  71.5 1.3 copy.250
  72.8 1.4 stack.23
  74.1 1.3 copy.251
  75.4 1.4 stack.24
  76.8 1.3 copy.252
  78.1 1.4 stack.25
  79.5 1.3 copy.253
  80.8 1.4 stack.26
  82.1 2.0 %convolution_bitcast_fusion = f32[4,3,128,128]{3,2,1,0:T(8,128)S(1)} fusion(f32[4,64,3,4]{1,0,2,3:T(4,128)} %copy.234, bf16[4,64,4,128,1]{3,2,1,0,4:T(4,128)(2,1)} %bitcast.379, bf16[4,64,4,128]{3,2,1,0:T(4,128)(2,1)S(1)} %reshape.222), kind=kOutput, calls=%fused_computation.5 | convolution fusion | flops 102760448 | bytes 1323008 | tf_op jit(solution)/shard_map/jchd,jclhe->lhde/dot_general | solution.py:26
  84.3 2.1 %fusion.173 = (bf16[3,4,128,128]{2,3,0,1:T(8,128)(2,1)}, f32[3,4,128,128]{2,3,0,1:T(8,128)}) fusion(f32[4,3,128,128]{3,2,1,0:T(8,128)S(1)} %convolution_bitcast_fusion, bf16[4,64,4,128,1]{3,2,1,0,4:T(4,128)(2,1)S(1)} %bitcast.380, f32[4,64,3,4]{1,0,2,3:T(4,128)S(1)} %copy-done.38, bf16[4,64,4,128]{3,2,1,0:T(4,128)(2,1)S(1)} %reshape.222), kind=kOutput, calls=%fused_computation.256 | convolution fusion | flops 101974016 | bytes 2502656 | tf_op jit(solution)/shard_map/jchd,jclhe->lhde/dot_general | solution.py:26
  88.5 1.4 fusion.3
  90.3 1.0 fusion.25
  92.4 1.0 fusion.79
  93.5 1.1 fusion.134
  94.5 1.0 fusion.101
  95.6 1.1 fusion.140
  96.7 1.1 fusion.105
  101.1 1.7 convolution_convert_fusion
  103.9 3.6 %fusion.16 = bf16[4,64,4,128]{3,1,2,0:T(8,128)(2,1)} fusion(f32[4,64,4,128]{3,1,2,0:T(8,128)S(1)} %bitcast.396, f32[4,4,64,128]{3,2,1,0:T(8,128)} %fusion.124, f32[4,128,4,64]{1,3,2,0:T(8,128)} %bitcast.391, f32[4,128,4,64]{1,3,2,0:T(8,128)} %bitcast.390, f32[4,128,4,64]{1,3,2,0:T(8,128)} %bitcast.393, f32[4,128,4,64]{1,3,2,0:T(8,128)} %bitcast.392, ...), kind=kOutput, calls=%fused_computation.31 | convolution fusion | flops 18743296 | bytes 5255168 | tf_op jit(solution)/shard_map/jhcs,jshd->jchd/dot_general | solution.py:21
  107.4 1.1 convert_element_type.313
  109.4 1.0 fusion.171
  110.9 28.4 %all-gather.1 = f32[8,16,4]{1,2,0:T(4,128)S(1)} all-gather(f32[1,16,4]{1,2,0:T(4,128)S(1)} %fusion.27), channel_id=2, replica_groups=mesh['seq'=8,'head'=4] {'seq'}, dimensions={0}, use_global_device_ids=true | all-gather | bytes 2304 | tf_op jit(solution)/shard_map/all_gather | solution.py:167
  139.9 2.0 %copy.275 = f32[2,1,4,128,128]{4,3,2,1,0:T(8,128)} copy(f32[2,1,4,128,128]{3,4,2,0,1:T(8,128)} %fusion.3) | data formatting | bytes 1048576
  141.9 2.1 %concatenate.23.clone = f32[2,2,4,128,128]{4,3,2,1,0:T(8,128)} pad(f32[2,1,4,128,128]{4,3,2,1,0:T(8,128)} %copy.275, f32[]{:T(128)} %constant.16.clone.1), padding=0_0x0_1x0_0x0_0x0_0 | pad | bytes 1572868 | tf_op jit(solution)/shard_map/concatenate | solution.py:54
  144.0 1.8 copy.231
  145.8 1.2 copy.221
  147.8 2.3 %fusion.48 = f32[4,4,128,64]{2,3,1,0:T(8,128)} fusion(f32[4,4,64,64]{3,2,1,0:T(8,128)S(1)} %convolution_multiply_fusion.1, f32[4,4,64]{2,1,0:T(4,128)S(1)} %get-tuple-element.41, bf16[4,64,4,128]{3,2,1,0:T(4,128)(2,1)} %copy-done.2), kind=kOutput, calls=%fused_computation.102 | convolution fusion | flops 16908288 | bytes 1052672 | tf_op jit(solution)/shard_map/jhcs,jche->jshe/dot_general | solution.py:21
  151.4 1.1 fusion.73
  152.5 5.6 %collective-permute-done.5 = bf16[1,4,128,128]{2,3,0,1:T(8,128)(2,1)S(1)} collective-permute-done((bf16[1,4,128,128]{2,3,0,1:T(8,128)(2,1)S(1)}, bf16[1,4,128,128]{2,3,0,1:T(8,128)(2,1)S(1)}, u32[]{:S(2)}, u32[]{:S(2)}) %collective-permute-start.5) | collective-permute-done | bytes 131104 | tf_op jit(solution)/shard_map/ppermute | solution.py:14
  158.0 1.7 fusion.61
  159.8 1.8 copy.237
  162.6 1.6 subtract_convert_fusion
  168.2 2.1 %copy.254 = f32[256,512]{1,0:T(8,128)} copy(f32[256,512]{0,1:T(8,128)} %reduce-scatter.5.cloned.1.call-done) | data formatting | bytes 1048576
  170.3 7.4 %reduce-scatter.3.cloned.1.call-done = bf16[256,512]{1,0:T(8,128)(2,1)} async-done(((bf16[256,2048]{1,0:T(8,128)(2,1)}), bf16[256,512]{1,0:T(8,128)(2,1)}) %reduce-scatter.3.cloned.1.call-update) | async-done | bytes 262160 | tf_op jit(solution)/shard_map/reduce_scatter | solution.py:142
  (190 shorter events, 31.4 us)
Async XLA Ops:
  7.2 43.1 %copy-start = (bf16[512,2048]{1,0:T(8,128)(2,1)S(1)}, bf16[512,2048]{1,0:T(8,128)(2,1)}, u32[]{:S(2)}) copy-start(bf16[512,2048]{1,0:T(8,128)(2,1)} %param.13) | copy-start | bytes 6291460
  7.2 7.5 %copy-start.23 = (bf16[256,512]{1,0:T(8,128)(2,1)S(1)}, bf16[256,512]{1,0:T(8,128)(2,1)}, u32[]{:S(2)}) copy-start(bf16[256,512]{1,0:T(8,128)(2,1)} %param.8) | copy-start | bytes 786436
  7.2 43.0 %all-gather.4.cloned.1.call-start = ((), (), s32[]{:S(2)}) async-start(), calls=%async_computation.3 | async-start | bytes 1310720 | tf_op jit(solution)/shard_map/all_gather | solution.py:107
  8.4 17.0 %copy-start.5 = (bf16[4,64,4,128]{3,2,1,0:T(4,128)(2,1)}, bf16[4,64,4,128]{3,2,1,0:T(4,128)(2,1)S(1)}, u32[]{:S(2)}) copy-start(bf16[4,64,4,128]{3,2,1,0:T(4,128)(2,1)S(1)} %reshape.213) | copy-start | bytes 786436
  10.9 3.8 %copy-start.14 = (f32[4,128,128]{2,1,0:T(8,128)}, f32[4,128,128]{2,1,0:T(8,128)S(1)}, u32[]{:S(2)}) copy-start(f32[4,128,128]{2,1,0:T(8,128)S(1)} %get-tuple-element.50) | copy-start | bytes 786436
  11.6 23.9 %collective-permute-start = (bf16[4,128,128]{2,1,0:T(8,128)(2,1)}, bf16[4,128,128]{2,1,0:T(8,128)(2,1)S(1)}, u32[]{:S(2)}, u32[]{:S(2)}) collective-permute-start(bf16[4,128,128]{2,1,0:T(8,128)(2,1)} %convert_element_type.273), channel_id=1, source_target_pairs={{0,4},{4,0},{8,12},{12,8},{16,20},{20,16},{24,28},{28,24},{1,5},{5... | collective-permute-start | bytes 393224 | tf_op jit(solution)/shard_map/ppermute | solution.py:14
  14.6 153.6 %reduce-scatter.5.cloned.1.call-start = ((), (), s32[]{:S(2)}) async-start(), calls=%async_computation.4 | async-start | bytes 4718592 | tf_op jit(solution)/shard_map/reduce_scatter | solution.py:146
  14.8 6.2 %copy-start.8 = (bf16[4,64,4,128]{3,2,1,0:T(4,128)(2,1)}, bf16[4,64,4,128]{3,2,1,0:T(4,128)(2,1)S(1)}, u32[]{:S(2)}) copy-start(bf16[4,64,4,128]{3,2,1,0:T(4,128)(2,1)S(1)} %reshape.212) | copy-start | bytes 786436
  17.4 8.0 %copy-start.12 = (f32[4,128,128]{2,1,0:T(8,128)}, f32[4,128,128]{2,1,0:T(8,128)S(1)}, u32[]{:S(2)}) copy-start(f32[4,128,128]{2,1,0:T(8,128)S(1)} %slice_reduce_fusion) | copy-start | bytes 786436
  18.5 1.8 copy-start.32
  22.0 3.4 %copy-start.18 = (bf16[2,1,64,4,128]{4,3,2,1,0:T(4,128)(2,1)}, bf16[2,1,64,4,128]{4,3,2,1,0:T(4,128)(2,1)S(1)}, u32[]{:S(2)}) copy-start(bf16[2,1,64,4,128]{4,3,2,1,0:T(4,128)(2,1)S(1)} %slice.119) | copy-start | bytes 393220
  22.0 5.7 %copy-start.51 = (s32[256,6]{0,1:T(8,128)S(1)}, s32[256,6]{0,1:T(8,128)}, u32[]{:S(2)}) copy-start(s32[256,6]{0,1:T(8,128)} %param.12) | copy-start | bytes 18436
  22.0 5.7 %copy-start.53 = (f32[16,4]{0,1:T(4,128)S(1)}, f32[16,4]{0,1:T(4,128)}, u32[]{:S(2)}) copy-start(f32[16,4]{0,1:T(4,128)} %param.11) | copy-start | bytes 772
  25.4 8.1 %copy-start.56 = (f32[6]{0:T(128)S(1)}, f32[6]{0:T(128)}, u32[]{:S(2)}) copy-start(f32[6]{0:T(128)} %constant.13.clone) | copy-start | bytes 76
  26.6 9.0 %copy-start.15 = (f32[4,128,128]{2,1,0:T(8,128)S(1)}, f32[4,128,128]{2,1,0:T(8,128)}, u32[]{:S(2)}) copy-start(f32[4,128,128]{2,1,0:T(8,128)} %copy-done.14) | copy-start | bytes 786436
  35.6 5.0 %collective-permute-start.1 = (bf16[4,128,128]{2,1,0:T(8,128)(2,1)S(1)}, bf16[4,128,128]{2,1,0:T(8,128)(2,1)S(1)}, u32[]{:S(2)}, u32[]{:S(2)}) collective-permute-start(bf16[4,128,128]{2,1,0:T(8,128)(2,1)S(1)} %fusion.78), channel_id=1, source_target_pairs={{0,8},{4,12},{8,0},{12,4},{16,24},{20,28},{24,16},{28,20},{1,9},{5... | collective-permute-start | bytes 393224 | tf_op jit(solution)/shard_map/ppermute | solution.py:14
  40.6 3.7 %copy-start.16 = (bf16[4,128,128]{2,1,0:T(8,128)(2,1)}, bf16[4,128,128]{2,1,0:T(8,128)(2,1)S(1)}, u32[]{:S(2)}) copy-start(bf16[4,128,128]{2,1,0:T(8,128)(2,1)S(1)} %collective-permute-done.1) | copy-start | bytes 393220
  40.7 7.5 %collective-permute-start.2 = (bf16[4,128,128]{2,1,0:T(8,128)(2,1)S(1)}, bf16[4,128,128]{2,1,0:T(8,128)(2,1)S(1)}, u32[]{:S(2)}, u32[]{:S(2)}) collective-permute-start(bf16[4,128,128]{2,1,0:T(8,128)(2,1)S(1)} %fusion.55), channel_id=1, source_target_pairs={{0,16},{4,20},{8,24},{12,28},{16,0},{20,4},{24,8},{28,12},{1,17},{... | collective-permute-start | bytes 393224 | tf_op jit(solution)/shard_map/ppermute | solution.py:14
  48.2 1.0 copy-start.27
  52.2 4.6 %copy-start.24 = (bf16[256,512]{1,0:T(8,128)(2,1)}, bf16[256,512]{1,0:T(8,128)(2,1)S(1)}, u32[]{:S(2)}) copy-start(bf16[256,512]{1,0:T(8,128)(2,1)S(1)} %convolution_convert_fusion.1) | copy-start | bytes 786436
  52.3 31.9 %copy-start.2 = (bf16[4,64,4,128]{3,2,1,0:T(4,128)(2,1)}, bf16[4,64,4,128]{3,2,1,0:T(4,128)(2,1)S(1)}, u32[]{:S(2)}) copy-start(bf16[4,64,4,128]{3,2,1,0:T(4,128)(2,1)S(1)} %reshape.222) | copy-start | bytes 786436
  52.3 4.7 %copy-start.34 = (bf16[256,2048]{1,0:T(8,128)(2,1)S(1)}, bf16[256,2048]{1,0:T(8,128)(2,1)}, u32[]{:S(2)}) copy-start(bf16[256,2048]{1,0:T(8,128)(2,1)} %all-gather.4.cloned.1.call-done) | copy-start | bytes 3145732
  57.0 2.7 %copy-start.20 = (bf16[4,64,4,128]{3,2,1,0:T(4,128)(2,1)}, bf16[4,64,4,128]{3,2,1,0:T(4,128)(2,1)S(1)}, u32[]{:S(2)}) copy-start(bf16[4,64,4,128]{3,2,1,0:T(4,128)(2,1)S(1)} %copy.197) | copy-start | bytes 786436
  59.8 4.8 %copy-start.25 = (bf16[256,512]{1,0:T(8,128)(2,1)S(1)}, bf16[256,512]{1,0:T(8,128)(2,1)}, u32[]{:S(2)}) copy-start(bf16[256,512]{1,0:T(8,128)(2,1)} %copy-done.24) | copy-start | bytes 786436
  59.8 117.9 %reduce-scatter.3.cloned.1.call-start = ((), (), s32[]{:S(2)}) async-start(), calls=%async_computation.2 | async-start | bytes 1310720 | tf_op jit(solution)/shard_map/reduce_scatter | solution.py:142
  82.1 2.1 %copy-start.9 = (bf16[4,64,4,128]{3,2,1,0:T(4,128)(2,1)S(1)}, bf16[4,64,4,128]{3,2,1,0:T(4,128)(2,1)}, u32[]{:S(2)}) copy-start(bf16[4,64,4,128]{3,2,1,0:T(4,128)(2,1)} %copy-done.8) | copy-start | bytes 786436
  82.1 2.1 %copy-start.38 = (f32[4,64,3,4]{1,0,2,3:T(4,128)S(1)}, f32[4,64,3,4]{1,0,2,3:T(4,128)}, u32[]{:S(2)}) copy-start(f32[4,64,3,4]{1,0,2,3:T(4,128)} %copy.234) | copy-start | bytes 36868
  82.1 5.1 %copy-start.36 = (bf16[2,2,64,4,128]{4,3,2,1,0:T(4,128)(2,1)S(1)}, bf16[2,2,64,4,128]{4,3,2,1,0:T(4,128)(2,1)}, u32[]{:S(2)}) copy-start(bf16[2,2,64,4,128]{4,3,2,1,0:T(4,128)(2,1)} %reshape_reshape.16) | copy-start | bytes 786436
  82.1 5.2 %copy-start.35 = (bf16[1,4,64,4,128]{4,3,2,1,0:T(4,128)(2,1)S(1)}, bf16[1,4,64,4,128]{4,3,2,1,0:T(4,128)(2,1)}, u32[]{:S(2)}) copy-start(bf16[1,4,64,4,128]{4,3,2,1,0:T(4,128)(2,1)} %reshape_reshape.17) | copy-start | bytes 786436
  84.2 3.2 %copy-start.46 = (f32[256,1,4]{0,2,1:T(4,128)S(1)}, f32[256,1,4]{0,2,1:T(4,128)}, u32[]{:S(2)}) copy-start(f32[256,1,4]{0,2,1:T(4,128)} %stack.21) | copy-start | bytes 12292
  84.2 3.2 %copy-start.47 = (f32[256,1,4]{0,2,1:T(4,128)S(1)}, f32[256,1,4]{0,2,1:T(4,128)}, u32[]{:S(2)}) copy-start(f32[256,1,4]{0,2,1:T(4,128)} %stack.22) | copy-start | bytes 12292
  84.2 3.2 %copy-start.48 = (f32[256,1,4]{0,2,1:T(4,128)S(1)}, f32[256,1,4]{0,2,1:T(4,128)}, u32[]{:S(2)}) copy-start(f32[256,1,4]{0,2,1:T(4,128)} %stack.23) | copy-start | bytes 12292
  84.2 3.2 %copy-start.49 = (f32[256,1,4]{0,2,1:T(4,128)S(1)}, f32[256,1,4]{0,2,1:T(4,128)}, u32[]{:S(2)}) copy-start(f32[256,1,4]{0,2,1:T(4,128)} %stack.24) | copy-start | bytes 12292
  84.3 3.2 %copy-start.50 = (f32[256,1,4]{0,2,1:T(4,128)S(1)}, f32[256,1,4]{0,2,1:T(4,128)}, u32[]{:S(2)}) copy-start(f32[256,1,4]{0,2,1:T(4,128)} %stack.25) | copy-start | bytes 12292
  84.3 3.3 %copy-start.33 = (bf16[1,2,64,4,128]{4,3,2,1,0:T(4,128)(2,1)S(1)}, bf16[1,2,64,4,128]{4,3,2,1,0:T(4,128)(2,1)}, u32[]{:S(2)}) copy-start(bf16[1,2,64,4,128]{4,3,2,1,0:T(4,128)(2,1)} %copy-done.32) | copy-start | bytes 393220
  84.3 3.3 %copy-start.44 = (f32[2,64,4]{1,0,2:T(2,128)S(1)}, f32[2,64,4]{1,0,2:T(2,128)}, u32[]{:S(2)}) copy-start(f32[2,64,4]{1,0,2:T(2,128)} %copy.430) | copy-start | bytes 6148
  84.3 3.6 %copy-start.19 = (bf16[2,1,64,4,128]{4,3,2,1,0:T(4,128)(2,1)S(1)}, bf16[2,1,64,4,128]{4,3,2,1,0:T(4,128)(2,1)}, u32[]{:S(2)}) copy-start(bf16[2,1,64,4,128]{4,3,2,1,0:T(4,128)(2,1)} %copy-done.18) | copy-start | bytes 393220
  86.4 3.5 %copy-start.13 = (f32[4,128,128]{2,1,0:T(8,128)S(1)}, f32[4,128,128]{2,1,0:T(8,128)}, u32[]{:S(2)}) copy-start(f32[4,128,128]{2,1,0:T(8,128)} %copy-done.12) | copy-start | bytes 786436
  86.4 21.1 %collective-permute-start.3 = (bf16[3,4,128,128]{2,3,0,1:T(8,128)(2,1)}, bf16[3,4,128,128]{2,3,0,1:T(8,128)(2,1)}, u32[]{:S(2)}, u32[]{:S(2)}) collective-permute-start(bf16[3,4,128,128]{2,3,0,1:T(8,128)(2,1)} %get-tuple-element.52), channel_id=1, source_target_pairs={{0,4},{4,0},{8,12},{12,8},{16,20},{20,16},{24,28},{28,24},{1,5},{5... | collective-permute-start | bytes 1179656 | tf_op jit(solution)/shard_map/ppermute | solution.py:14
  87.9 3.4 %copy-start.43 = (f32[2,64,4]{1,2,0:T(4,128)S(1)}, f32[2,64,4]{1,2,0:T(4,128)}, u32[]{:S(2)}) copy-start(f32[2,64,4]{1,2,0:T(4,128)} %slice_bitcast_fusion.7) | copy-start | bytes 6148
  88.4 3.7 %copy-start.1 = (f32[4,4,128,128]{3,2,1,0:T(8,128)S(1)}, f32[4,4,128,128]{3,2,1,0:T(8,128)}, u32[]{:S(2)}) copy-start(f32[4,4,128,128]{3,2,1,0:T(8,128)} %get-tuple-element.51) | copy-start | bytes 3145732
  89.8 2.6 %copy-start.28 = (bf16[4,128,128]{2,1,0:T(8,128)(2,1)S(1)}, bf16[4,128,128]{2,1,0:T(8,128)(2,1)}, u32[]{:S(2)}) copy-start(bf16[4,128,128]{2,1,0:T(8,128)(2,1)} %copy-done.27) | copy-start | bytes 393220
  90.3 4.3 %copy-start.17 = (bf16[4,128,128]{2,1,0:T(8,128)(2,1)S(1)}, bf16[4,128,128]{2,1,0:T(8,128)(2,1)}, u32[]{:S(2)}) copy-start(bf16[4,128,128]{2,1,0:T(8,128)(2,1)} %copy-done.16) | copy-start | bytes 393220
  93.5 5.3 %copy-start.3 = (bf16[4,64,4,128]{3,2,1,0:T(4,128)(2,1)S(1)}, bf16[4,64,4,128]{3,2,1,0:T(4,128)(2,1)}, u32[]{:S(2)}) copy-start(bf16[4,64,4,128]{3,2,1,0:T(4,128)(2,1)} %copy-done.2) | copy-start | bytes 786436
  93.5 5.3 %copy-start.37 = (f32[64,64]{1,0:T(8,128)S(1)}, f32[64,64]{1,0:T(8,128)}, u32[]{:S(2)}) copy-start(f32[64,64]{1,0:T(8,128)} %fusion.146) | copy-start | bytes 49156
  95.6 3.5 %copy-start.42 = (f32[2,64,4]{1,2,0:T(4,128)S(1)}, f32[2,64,4]{1,2,0:T(4,128)}, u32[]{:S(2)}) copy-start(f32[2,64,4]{1,2,0:T(4,128)} %slice_bitcast_fusion.8) | copy-start | bytes 6148
  96.7 3.4 %copy-start.6 = (bf16[4,64,4,128]{3,2,1,0:T(4,128)(2,1)S(1)}, bf16[4,64,4,128]{3,2,1,0:T(4,128)(2,1)}, u32[]{:S(2)}) copy-start(bf16[4,64,4,128]{3,2,1,0:T(4,128)(2,1)} %copy-done.5) | copy-start | bytes 786436
  97.8 3.3 %copy-start.21 = (bf16[4,64,4,128]{3,2,1,0:T(4,128)(2,1)S(1)}, bf16[4,64,4,128]{3,2,1,0:T(4,128)(2,1)}, u32[]{:S(2)}) copy-start(bf16[4,64,4,128]{3,2,1,0:T(4,128)(2,1)} %copy-done.20) | copy-start | bytes 786436
  100.1 2.7 %copy-start.45 = (f32[256,1,4]{0,2,1:T(4,128)S(1)}, f32[256,1,4]{0,2,1:T(4,128)}, u32[]{:S(2)}) copy-start(f32[256,1,4]{0,2,1:T(4,128)} %stack.26) | copy-start | bytes 12292
  100.1 2.7 %copy-start.55 = (f32[256,6,4]{0,2,1:T(4,128)S(1)}, f32[256,6,4]{0,2,1:T(4,128)}, u32[]{:S(2)}) copy-start(f32[256,6,4]{0,2,1:T(4,128)} %copy-done.54) | copy-start | bytes 73732
  101.1 2.7 %copy-start.39 = (f32[4,64,4]{1,2,0:T(4,128)S(1)}, f32[4,64,4]{1,2,0:T(4,128)}, u32[]{:S(2)}) copy-start(f32[4,64,4]{1,2,0:T(4,128)} %get-tuple-element.36) | copy-start | bytes 12292
  101.1 2.7 %copy-start.40 = (f32[4,64,4]{1,2,0:T(4,128)S(1)}, f32[4,64,4]{1,2,0:T(4,128)}, u32[]{:S(2)}) copy-start(f32[4,64,4]{1,2,0:T(4,128)} %get-tuple-element.37) | copy-start | bytes 12292
  101.1 2.7 %copy-start.41 = (f32[4,64,4]{1,2,0:T(4,128)S(1)}, f32[4,64,4]{1,2,0:T(4,128)}, u32[]{:S(2)}) copy-start(f32[4,64,4]{1,2,0:T(4,128)} %get-tuple-element.38) | copy-start | bytes 12292
  103.8 5.5 %copy-start.26 = (f32[3,4,128,128]{2,3,0,1:T(8,128)S(1)}, f32[3,4,128,128]{2,3,0,1:T(8,128)}, u32[]{:S(2)}) copy-start(f32[3,4,128,128]{2,3,0,1:T(8,128)} %get-tuple-element.53) | copy-start | bytes 2359300
  107.4 3.3 %copy-start.52 = (s32[256,6]{0,1:T(8,128)S(1)}, s32[256,6]{0,1:T(8,128)}, u32[]{:S(2)}) copy-start(s32[256,6]{0,1:T(8,128)} %param.12) | copy-start | bytes 18436
  110.4 39.6 %collective-permute-start.4 = (bf16[2,4,128,128]{2,3,0,1:T(8,128)(2,1)}, bf16[2,4,128,128]{2,3,0,1:T(8,128)(2,1)}, u32[]{:S(2)}, u32[]{:S(2)}) collective-permute-start(bf16[2,4,128,128]{2,3,0,1:T(8,128)(2,1)} %get-tuple-element.30), channel_id=1, source_target_pairs={{0,8},{4,12},{8,0},{12,4},{16,24},{20,28},{24,16},{28,20},{1,9},{5... | collective-permute-start | bytes 786440 | tf_op jit(solution)/shard_map/ppermute | solution.py:14
  147.7 3.3 %copy-start.31 = (f32[2,4,128,128]{2,3,0,1:T(8,128)S(1)}, f32[2,4,128,128]{2,3,0,1:T(8,128)}, u32[]{:S(2)}) copy-start(f32[2,4,128,128]{2,3,0,1:T(8,128)} %get-tuple-element.31) | copy-start | bytes 1572868
  147.7 3.6 %copy-start.10 = (bf16[4,64,4,128]{3,2,1,0:T(4,128)(2,1)S(1)}, bf16[4,64,4,128]{3,2,1,0:T(4,128)(2,1)}, u32[]{:S(2)}) copy-start(bf16[4,64,4,128]{3,2,1,0:T(4,128)(2,1)} %copy-done.8) | copy-start | bytes 786436
  151.1 7.0 %collective-permute-start.5 = (bf16[1,4,128,128]{2,3,0,1:T(8,128)(2,1)S(1)}, bf16[1,4,128,128]{2,3,0,1:T(8,128)(2,1)S(1)}, u32[]{:S(2)}, u32[]{:S(2)}) collective-permute-start(bf16[1,4,128,128]{2,3,0,1:T(8,128)(2,1)S(1)} %fusion.58), channel_id=1, source_target_pairs={{0,16},{4,20},{8,24},{12,28},{16,0},{20,4},{24,8},{28,12},{1,17},{... | collective-permute-start | bytes 393224 | tf_op jit(solution)/shard_map/ppermute | solution.py:14
  164.2 1.0 copy-start.11
  164.2 1.1 copy-start.30
  164.6 1.2 copy-start.7
  165.6 1.0 copy-start.4
  165.6 1.1 copy-start.29
  (2 other events, 1.8 us)
Sparse Core Ops, SparseCore 0:
  14.7 17.0 all-gather.3
  59.9 88.4 reduce-scatter.4
  151.6 26.0 reduce-scatter.2
